TPU v7x, 32 devices: a whole 2x2x4 slice. The times are simulated.
32 devices in a mesh: dp: 2 (over core), shard: 16 (over z, y, x).
Axes of the slice: x: 2, y: 2, z: 4, core: 2. Of those that a mesh axis runs over, the one named last changes fastest.
Arguments:
- hidden_in: bfloat16 [4096, 1024], P(('dp', 'shard')), may hold values from -6 to 6
- doc_ids: int32 [32, 128], P(('dp', 'shard')), may hold values from 0 to 3, never falling along the last dimension, each value on 1 to 64 neighbouring positions
- expert_ids: int32 [4096], P(('dp', 'shard')), may hold values from 0 to 1, as said below
- slot_ids: int32 [4096], P(('dp', 'shard')), may hold values from 0 to 73, as said below
- out_grad: bfloat16 [4096, 1024], P(('dp', 'shard')), may hold values from -6 to 6
- ln1_gain: bfloat16 [1024], P(('dp', 'shard')), may hold values from 0.5 to 1.5
- ln1_bias: bfloat16 [1024], P(('dp', 'shard')), may hold values from -1 to 1
- w_query: bfloat16 [1024, 1024], P(('dp', 'shard')), may hold values from -0.1875 to 0.1875
- w_key: bfloat16 [1024, 1024], P(('dp', 'shard')), may hold values from -0.1875 to 0.1875
- w_value: bfloat16 [1024, 1024], P(('dp', 'shard')), may hold values from -0.1875 to 0.1875
- w_out: bfloat16 [1024, 1024], P(('dp', 'shard')), may hold values from -0.5 to 0.5
- ln2_gain: bfloat16 [1024], P(('dp', 'shard')), may hold values from 0.5 to 1.5
- ln2_bias: bfloat16 [1024], P(('dp', 'shard')), may hold values from -1 to 1
- w_up: bfloat16 [1024, 4096], P(('dp', 'shard')), may hold values from -0.1875 to 0.1875
- w_down: bfloat16 [4096, 1024], P(('dp', 'shard')), may hold values from -0.09375 to 0.09375
- w_router: bfloat16 [1024, 2], P(('dp', 'shard')), may hold values from -0.125 to 0.125
- w_mix: bfloat16 [1024, 2], P(('dp', 'shard')), may hold values from -0.1875 to 0.1875
- expert_up: bfloat16 [2, 1024, 4096], P(None, ('dp', 'shard')), may hold values from -0.1875 to 0.1875
- expert_down: bfloat16 [2, 4096, 1024], P(None, ('dp', 'shard')), may hold values from -0.09375 to 0.09375
- load_avg: float32 [2], replicated, may hold values from 0.05 to 0.3
Outputs:
- layer_out: bfloat16 [4096, 1024], P(('dp', 'shard'))
- input_grad: bfloat16 [4096, 1024], P(('dp', 'shard'))
- grad_ln1_gain: float32 [1024], P(('dp', 'shard'))
- grad_ln1_bias: float32 [1024], P(('dp', 'shard'))
- grad_w_query: float32 [1024, 1024], P(('dp', 'shard'))
- grad_w_key: float32 [1024, 1024], P(('dp', 'shard'))
- grad_w_value: float32 [1024, 1024], P(('dp', 'shard'))
- grad_w_out: float32 [1024, 1024], P(('dp', 'shard'))
- grad_ln2_gain: float32 [1024], P(('dp', 'shard'))
- grad_ln2_bias: float32 [1024], P(('dp', 'shard'))
- grad_w_up: float32 [1024, 4096], P(('dp', 'shard'))
- grad_w_down: float32 [4096, 1024], P(('dp', 'shard'))
- grad_w_router: float32 [1024, 2], P(('dp', 'shard'))
- grad_w_mix: float32 [1024, 2], P(('dp', 'shard'))
- grad_expert_up: float32 [2, 1024, 4096], P(None, ('dp', 'shard'))
- grad_expert_down: float32 [2, 4096, 1024], P(None, ('dp', 'shard'))
- expert_counts: int32 [2], replicated
- load_avg_new: float32 [2], replicated
Inputs may be any that keep to these rules, and one draw needn't show every extreme that they name: `expert_ids`: of the 128 tokens of one sequence at most 74 go to one expert, and in some sequence exactly 74 do. `slot_ids`: A token's slot is the number of earlier tokens of the same sequence routed to the same expert.
All inputs are finite; a program needn't handle non-finite values.
Results may differ from a plain program's by a relative error of at most 0.012.
The roundings to bfloat16 on the way count: a program that leaves them out, or rounds other values in their place, can miss the bound.
Values may be sent and summed in bfloat16 or wider, within the bound.
A program may use at most 384 MiB of HBM per device.

v0:
```python
import jax
import jax.numpy as jnp
from jax import lax
from jax.sharding import PartitionSpec as P

HEADS = 16
CAP = 74
BF = jnp.bfloat16
F32 = jnp.float32
BOTH = ("dp", "shard")


def mm(a, b, dims=((1,), (0,))):
    return lax.dot_general(a, b, (dims, ((), ())), preferred_element_type=F32)


def layer_norm(values, gain, bias):
    centre = values - jnp.mean(values, axis=-1, keepdims=True)
    scale_inv = lax.rsqrt(jnp.mean(centre * centre, axis=-1, keepdims=True) + 1e-05)
    normed = centre * scale_inv
    return (normed * gain + bias, normed, scale_inv)


def norm_back(grad_out, normed, scale_inv, gain):
    grad_normed = grad_out * gain
    inner = grad_normed - jnp.mean(grad_normed, axis=-1, keepdims=True)
    inner = inner - normed * jnp.mean(grad_normed * normed, axis=-1, keepdims=True)
    return (scale_inv * inner, jnp.sum(grad_out * normed, axis=0), jnp.sum(grad_out, axis=0))


def gelu_pair(t):
    inner = 0.7978845608 * (t + 0.044715 * t * t * t)
    th = jnp.tanh(inner)
    val = 0.5 * t * (1.0 + th)
    der = 0.5 * (1.0 + th) + 0.5 * t * (1.0 - th * th) * 0.7978845608 * (
        1.0 + 3.0 * 0.044715 * t * t
    )
    return (val, der)


def ag(block):
    return lax.all_gather(block, "shard", axis=0, tiled=False)


def rs(parts):
    return lax.psum_scatter(parts.astype(BF), "shard", scatter_dimension=0, tiled=False).astype(F32)


def body(
    hidden_in,
    doc_ids,
    expert_ids,
    slot_ids,
    out_grad,
    ln1_gain,
    ln1_bias,
    w_query,
    w_key,
    w_value,
    w_out,
    ln2_gain,
    ln2_bias,
    w_up,
    w_down,
    w_router,
    w_mix,
    expert_up,
    expert_down,
    load_avg,
):
    T, D = hidden_in.shape
    H, HD = (HEADS, D // HEADS)
    S = lax.axis_size("shard")
    C = lax.axis_size("dp")
    WR = w_query.shape[0]
    FF = w_up.shape[1]
    FR = w_down.shape[0]
    F = FR * C
    E = expert_up.shape[0]
    LO, HI = (80, T - 80)
    pos = jnp.where(
        expert_ids == 0, slot_ids, jnp.sum((expert_ids == 0).astype(jnp.int32)) + slot_ids
    )
    n0 = jnp.sum((expert_ids == 0).astype(jnp.int32))
    place = lax.iota(jnp.int32, T)
    perm = (pos[None, :] == place[:, None]).astype(BF)
    xs = mm(perm, hidden_in)
    dys = mm(perm, out_grad).astype(BF)
    doc = doc_ids[0]
    allowed = (place[None, :] <= place[:, None]) & (doc[:, None] == doc[None, :])
    allowed = mm(mm(perm, allowed.astype(BF)).astype(BF), perm, ((1,), (1,))) > 0.5
    is0 = (place < n0)[:, None]
    small = jnp.stack(
        [
            ln1_gain,
            ln1_bias,
            ln2_gain,
            ln2_bias,
            w_router[:, 0],
            w_router[:, 1],
            w_mix[:, 0],
            w_mix[:, 1],
        ]
    ).astype(F32)
    small = lax.all_gather(small, BOTH, axis=1, tiled=True)
    g1, b1, g2, b2 = (small[0], small[1], small[2], small[3])
    wr, wm = (small[4:6], small[6:8])
    wa = jnp.stack([w_query, w_key, w_value, w_out])
    wa = lax.all_gather(wa, BOTH, axis=1, tiled=True)
    wq, wk, wv, wo = (wa[0], wa[1], wa[2], wa[3])
    ups = jnp.stack([w_up, expert_up[0], expert_up[1]])
    ups = ups.reshape(3, WR, C, S, FR).transpose(3, 0, 1, 2, 4).reshape(S, 3, WR, F)
    ups = lax.all_to_all(ups, "shard", 0, 0)
    ups = lax.all_gather(ups, "dp", axis=0)
    ups = ups.transpose(2, 0, 1, 3, 4).reshape(3, D, F)
    downs = jnp.stack([w_down, expert_down[0], expert_down[1]])
    downs = lax.all_gather(downs, "dp", axis=1, tiled=True)
    dy_all = ag(dys)
    n1, u1, i1 = layer_norm(xs, g1, b1)
    h1b = n1.astype(BF)
    q = (mm(h1b, wq) * 0.125).astype(BF).reshape(T, H, HD)
    k = mm(h1b, wk).astype(BF).reshape(T, H, HD)
    v = mm(h1b, wv).astype(BF).reshape(T, H, HD)
    s = jnp.einsum("ihd,jhd->hij", q, k, preferred_element_type=F32)
    s = jnp.where(allowed[None], s, -1e30)
    ex = jnp.exp(s - jnp.max(s, axis=-1, keepdims=True))
    p = ex / jnp.sum(ex, axis=-1, keepdims=True)
    pb = p.astype(BF)
    o = jnp.einsum("hij,jhd->ihd", pb, v, preferred_element_type=F32).reshape(T, D).astype(BF)
    x1 = xs + mm(o, wo)
    h2, u2, i2 = layer_norm(x1, g2, b2)
    h2b = h2.astype(BF)

    def two(w):
        return jnp.stack([jnp.sum(h2 * w[0], axis=-1), jnp.sum(h2 * w[1], axis=-1)], axis=-1)

    r = jax.nn.softmax(two(wr), axis=-1)
    c = jax.nn.softmax(two(wm), axis=-1)
    gate = jnp.where(is0, r[:, 0:1], r[:, 1:2])
    c0, c1 = (c[:, 0:1], c[:, 1:2])
    we = c0 * gate
    scal = jnp.concatenate([c1, jnp.where(is0, we, 0.0), jnp.where(is0, 0.0, we)], axis=1)
    h_all = ag(h2b)
    scal_all = ag(scal)

    def cut(a, e):
        return (a[:, :LO] if e == 1 else a[:, HI:]) if e else a

    partial_y = jnp.zeros((S, T, D), F32)
    partial_dh = jnp.zeros((S, T, D), F32)
    score = []
    gup, gdown = ([], [])
    for e in range(3):
        he = cut(h_all, e)
        dye = cut(dy_all, e).astype(F32)
        se = cut(scal_all, e)[:, :, e : e + 1]
        n = he.shape[1]
        hf = he.reshape(S * n, D)
        pre = mm(hf, ups[e])
        val, der = gelu_pair(pre)
        ub = val.astype(BF)
        m = mm(ub, downs[e]).reshape(S, n, D)
        dm = (dye * se).astype(BF).reshape(S * n, D)
        dg = (mm(dm, downs[e], ((1,), (1,))) * der).astype(BF)
        gdown.append(mm(ub, dm, ((0,), (0,))))
        gup.append(mm(hf, dg, ((0,), (0,))))
        dx = mm(dg, ups[e], ((1,), (1,))).reshape(S, n, D)
        y = m * se
        sc = jnp.sum(dye * m, axis=-1)
        pad = [(0, 0), (0, T - n) if e < 2 else (T - n, 0)]
        live = is0[None, :, 0]
        partial_y += jnp.pad(y, pad + [(0, 0)])
        partial_dh += jnp.pad(dx, pad + [(0, 0)])
        score.append(jnp.pad(sc, pad))
    yfull = rs(partial_y)
    dh2 = rs(partial_dh)
    sc = lax.psum_scatter(jnp.stack(score, axis=1), "shard", scatter_dimension=0, tiled=False)
    sm = sc[0][:, None]
    se = jnp.where(is0, sc[1][:, None], sc[2][:, None])
    dc0, dc1 = (gate * se, sm)
    tot = c0 * dc0 + c1 * dc1
    dcl0, dcl1 = (c0 * (dc0 - tot), c1 * (dc1 - tot))
    dgate = c0 * se
    dr0, dr1 = (jnp.where(is0, dgate, 0.0), jnp.where(is0, 0.0, dgate))
    tot = r[:, 0:1] * dr0 + r[:, 1:2] * dr1
    drl0, drl1 = (r[:, 0:1] * (dr0 - tot), r[:, 1:2] * (dr1 - tot))
    layer_out = (x1 + yfull).astype(BF)
    dh2 = dh2 + drl0 * wr[0] + drl1 * wr[1] + dcl0 * wm[0] + dcl1 * wm[1]
    gw = [jnp.sum(h2 * t, axis=0) for t in (drl0, drl1, dcl0, dcl1)]
    dx1, gg2, gb2 = norm_back(dh2, u2, i2, g2)
    dx1 = dx1 + dys.astype(F32)
    dab = dx1.astype(BF)
    gwo = mm(o, dab, ((0,), (0,)))
    do = mm(dab, wo, ((1,), (1,))).astype(BF).reshape(T, H, HD)
    dp = jnp.einsum("ihd,jhd->hij", do, v, preferred_element_type=F32)
    ds = (p * (dp - jnp.sum(p * dp, axis=-1, keepdims=True))).astype(BF)
    dq = jnp.einsum("hij,jhd->ihd", ds, k, preferred_element_type=F32).astype(BF)
    dq = (dq * BF(0.125)).reshape(T, D)
    dk = jnp.einsum("hij,ihd->jhd", ds, q, preferred_element_type=F32).astype(BF).reshape(T, D)
    dv = jnp.einsum("hij,ihd->jhd", pb, do, preferred_element_type=F32).astype(BF).reshape(T, D)
    dh1 = mm(dq, wq, ((1,), (1,))) + mm(dk, wk, ((1,), (1,))) + mm(dv, wv, ((1,), (1,)))
    ga = jnp.stack(
        [mm(h1b, dq, ((0,), (0,))), mm(h1b, dk, ((0,), (0,))), mm(h1b, dv, ((0,), (0,))), gwo]
    )
    dxn, gg1, gb1 = norm_back(dh1, u1, i1, g1)
    input_grad = (dx1 + dxn).astype(BF)
    layer_out = mm(perm, layer_out, ((0,), (0,))).astype(BF)
    input_grad = mm(perm, input_grad, ((0,), (0,))).astype(BF)
    smalls = lax.psum(jnp.stack([gg1, gb1, gg2, gb2] + gw), BOTH)
    mine = lax.dynamic_slice_in_dim(smalls, lax.axis_index(BOTH) * WR, WR, 1)
    ga = ga.reshape(4, C, S, WR, D).transpose(1, 2, 0, 3, 4)
    ga = lax.psum_scatter(ga.astype(BF), "dp", scatter_dimension=0, tiled=False)
    ga = lax.psum_scatter(ga, "shard", scatter_dimension=0, tiled=False).astype(F32)
    gdown = lax.psum_scatter(jnp.stack(gdown), "dp", scatter_dimension=1, tiled=True)
    gup = jnp.stack(gup).reshape(3, C, S, WR, F).transpose(1, 2, 0, 3, 4)
    gup = lax.psum_scatter(gup, "dp", scatter_dimension=0, tiled=False).astype(BF)
    gup = lax.all_to_all(gup, "shard", 0, 0).astype(F32)
    gup = gup.reshape(S, 3, WR, C, FR).transpose(1, 2, 3, 0, 4).reshape(3, WR, FF)
    counts = lax.psum(jnp.stack([n0, T - n0]), BOTH)
    load_new = 0.9 * load_avg + 0.1 * counts.astype(F32) * E / (T * C * S)
    return (
        layer_out,
        input_grad,
        mine[0],
        mine[1],
        ga[0],
        ga[1],
        ga[2],
        ga[3],
        mine[2],
        mine[3],
        gup[0],
        gdown[0],
        jnp.stack([mine[4], mine[5]], axis=1),
        jnp.stack([mine[6], mine[7]], axis=1),
        gup[1:],
        gdown[1:],
        counts,
        load_new,
    )


def solution(mesh):
    row, vec = (P(BOTH, None), P(BOTH))
    mid = P(None, BOTH, None)
    return jax.shard_map(
        body,
        mesh=mesh,
        in_specs=(
            row,
            row,
            vec,
            vec,
            row,
            vec,
            vec,
            row,
            row,
            row,
            row,
            vec,
            vec,
            row,
            row,
            row,
            row,
            mid,
            mid,
            P(),
        ),
        out_specs=(
            row,
            row,
            vec,
            vec,
            row,
            row,
            row,
            row,
            vec,
            vec,
            row,
            row,
            row,
            row,
            mid,
            mid,
            P(),
            P(),
        ),
        check_vma=False,
    )
```

profile of v0, /device:TPU:0, one launch (start us, length us, event | category | flops | bytes accessed | tf_op | source)
XLA Modules:
  0.0 906.7 jit_solution(14686394213423674145)
XLA Ops:
  13.6 8.3 all-to-all-start
  22.1 81.6 %all-gather.4 = f32[32,32,8]{1,2,0:T(8,128)S(1)} all-gather(f32[1,32,8]{1,2,0:T(8,128)S(1)} %convert_bitcast_fusion.4), channel_id=1, replica_groups=mesh['dp'=2,'shard'=16] {'dp','shard'}, dimensions={0}, use_global_device_ids=true | all-gather | bytes 33792 | tf_op jit(solution)/shard_map/all_gather | solution.py:105
  125.9 70.1 %all-gather.15.cloned.1.call-done = bf16[2048,1024]{1,0:T(8,128)(2,1)} async-done(((bf16[128,1024]{1,0:T(8,128)(2,1)}), bf16[2048,1024]{1,0:T(8,128)(2,1)}) %all-gather.15.cloned.1.call-update) | async-done | bytes 4194320 | tf_op jit(solution)/shard_map/all_gather | solution.py:42
  196.0 3.2 fusion.113
  199.2 2.8 multiply_convert_fusion.1
  205.8 4.4 fusion.52
  210.2 76.1 %all-gather.19.cloned.1.call-done = bf16[2048,1024]{1,0:T(8,128)(2,1)} async-done(((bf16[128,1024]{1,0:T(8,128)(2,1)}), bf16[2048,1024]{1,0:T(8,128)(2,1)}) %all-gather.19.cloned.1.call-update) | async-done | bytes 4194320 | tf_op jit(solution)/shard_map/all_gather | solution.py:42
  286.3 8.0 fusion.4
  294.4 2.9 multiply_convert_fusion
  297.4 6.0 fusion.2
  303.4 74.4 %all-reduce.6 = f32[16,3,128]{2,1,0:T(4,128)S(1)} all-reduce(f32[16,3,128]{2,1,0:T(4,128)S(1)} %pad_maximum_fusion.3), channel_id=8, replica_groups=mesh['dp'=2,'shard'=16] {'shard'}, use_global_device_ids=true, to_apply=%region_18.19.clone | all-reduce | flops 6144 | bytes 49152
  380.5 35.8 %all-gather.2 = f32[2048,3]{0,1:T(4,128)S(1)} all-gather(f32[128,3]{0,1:T(4,128)S(1)} %pad_maximum_fusion.4), channel_id=4, replica_groups=mesh['dp'=2,'shard'=16] {'shard'}, dimensions={0}, use_global_device_ids=true | all-gather | bytes 26112 | tf_op jit(solution)/shard_map/all_gather | solution.py:42
  416.4 10.2 %fusion.3 = (bf16[16,80,1024]{2,1,0:T(8,128)(2,1)S(1)}, bf16[16,80,1024]{2,1,0:T(8,128)(2,1)S(1)}, f32[16,80,1024]{2,1,0:T(8,128)}, f32[16,80,1024]{2,1,0:T(8,128)}) fusion(f32[16,80]{1,0:T(8,128)S(1)} %get-tuple-element.62, bf16[16,128,1024]{2,1,0:T(8,128)(2,1)} %bitcast.390, f32[16,80]{1,0:T(8,128)S(1)} %get-tuple-element.63, f32[16,80,1024]{2,1,0:T(8,128)} %fusion.52, ...), kind=kLoop, calls=%fused_computation.12 | loop fusion | flops 10485760 | bytes 31467520 | tf_op jit(solution)/shard_map/convert_element_type | solution.py:163
  428.0 3.2 fusion.119
  432.7 3.5 fusion.120
  438.2 7.0 fusion.1
  445.2 5.2 fusion.7
  451.4 2.9 add_convert_fusion
  454.9 92.5 %reduce-scatter.15.cloned.1.call-done = bf16[1,128,1024]{2,1,0:T(8,128)(2,1)} async-done(((bf16[16,128,1024]{2,1,0:T(8,128)(2,1)}), bf16[1,128,1024]{2,1,0:T(8,128)(2,1)}) %reduce-scatter.15.cloned.1.call-update) | async-done | bytes 262160 | tf_op jit(solution)/shard_map/reduce_scatter | solution.py:46
  560.0 3.8 maximum_bitcast_fusion
  563.9 3.0 convolution_bitcast_fusion
  574.0 4.6 copy.102
  578.7 4.4 copy.103
  583.1 6.6 copy.101
  589.7 3.3 convolution_bitcast_fusion.4
  599.3 12.2 %all-reduce.17 = bf16[2,16,3,32,256]{4,3,1,0,2:T(8,128)(2,1)S(1)} all-reduce(f32[2,16,3,32,256]{4,3,1,0,2:T(8,128)} %maximum_bitcast_fusion.1), channel_id=11, replica_groups=mesh['dp'=2,'shard'=16] {'dp'}, use_global_device_ids=true, to_apply=%region_35.36.clone | all-reduce | flops 786432 | bytes 4718592
  613.2 5.7 all-to-all-start.1
  619.0 5.6 dynamic-slice_bitcast_fusion
  626.0 48.3 %psum.15 = s32[2]{0:T(128)S(1)} all-reduce(s32[2]{0:T(128)S(1)} %pad_add_fusion), channel_id=1, replica_groups=mesh['dp'=2,'shard'=16] {'dp','shard'}, use_global_device_ids=true, to_apply=%region_37.38 | all-reduce | flops 2 | bytes 16 | tf_op jit(solution)/shard_map/psum | solution.py:219
  690.0 2.6 multiply_reduce_fusion.6
  692.7 43.1 %psum.14 = f32[8,1024]{1,0:T(8,128)S(1)} all-reduce(f32[8,1024]{1,0:T(8,128)S(1)} %stack.176), channel_id=1, replica_groups=mesh['dp'=2,'shard'=16] {'dp','shard'}, use_global_device_ids=true, to_apply=%region_32.33 | all-reduce | flops 8192 | bytes 65536 | tf_op jit(solution)/shard_map/psum | solution.py:209
  740.6 156.4 %all-reduce.16.cloned.1.call-done = bf16[16,4,32,1024]{3,2,0,1:T(8,128)(2,1)} async-done(((bf16[16,4,32,1024]{3,2,0,1:T(8,128)(2,1)}), bf16[16,4,32,1024]{3,2,0,1:T(8,128)(2,1)}) %all-reduce.16.cloned.1.call-update) | async-done | bytes 4194320
  (271 shorter events, 92.6 us)
Async XLA Ops:
  7.2 98.4 %copy-start = (bf16[128,1024]{1,0:T(8,128)(2,1)S(1)}, bf16[128,1024]{1,0:T(8,128)(2,1)}, u32[]{:S(2)}) copy-start(bf16[128,1024]{1,0:T(8,128)(2,1)} %param.20) | copy-start | bytes 786436
  7.2 100.0 %all-gather.11.cloned.1.call-start = ((), (), s32[]{:S(2)}) async-start(), calls=%async_computation.5 | async-start | bytes 8650752 | tf_op jit(solution)/shard_map/all_gather | solution.py:109
  11.0 10.9 %copy-start.44 = (bf16[32,2]{0,1:T(2,128)(2,1)S(1)}, bf16[32,2]{0,1:T(2,128)(2,1)}, u32[]{:S(2)}) copy-start(bf16[32,2]{0,1:T(2,128)(2,1)} %param.36) | copy-start | bytes 388
  11.1 10.9 %copy-start.45 = (bf16[32,2]{0,1:T(2,128)(2,1)S(1)}, bf16[32,2]{0,1:T(2,128)(2,1)}, u32[]{:S(2)}) copy-start(bf16[32,2]{0,1:T(2,128)(2,1)} %param.35) | copy-start | bytes 388
  11.1 10.9 %copy-start.46 = (bf16[32]{0:T(256)(128)(2,1)S(1)}, bf16[32]{0:T(256)(128)(2,1)}, u32[]{:S(2)}) copy-start(bf16[32]{0:T(256)(128)(2,1)} %param.25) | copy-start | bytes 196
  11.1 10.9 %copy-start.47 = (bf16[32]{0:T(256)(128)(2,1)S(1)}, bf16[32]{0:T(256)(128)(2,1)}, u32[]{:S(2)}) copy-start(bf16[32]{0:T(256)(128)(2,1)} %param.26) | copy-start | bytes 196
  11.1 10.9 %copy-start.48 = (bf16[32]{0:T(256)(128)(2,1)S(1)}, bf16[32]{0:T(256)(128)(2,1)}, u32[]{:S(2)}) copy-start(bf16[32]{0:T(256)(128)(2,1)} %param.31) | copy-start | bytes 196
  11.1 10.9 %copy-start.49 = (bf16[32]{0:T(256)(128)(2,1)S(1)}, bf16[32]{0:T(256)(128)(2,1)}, u32[]{:S(2)}) copy-start(bf16[32]{0:T(256)(128)(2,1)} %param.32) | copy-start | bytes 196
  12.1 91.7 %copy-start.51 = (s32[128]{0:T(128)S(1)}, s32[128]{0:T(128)}, u32[]{:S(2)}) copy-start(s32[128]{0:T(128)} %param.22) | copy-start | bytes 1540
  12.2 92.3 %copy-start.50 = (s32[128]{0:T(128)S(1)}, s32[128]{0:T(128)}, u32[]{:S(2)}) copy-start(s32[128]{0:T(128)} %param.23) | copy-start | bytes 1540
  12.2 93.0 %copy-start.52 = (s32[1,128]{1,0:T(1,128)S(1)}, s32[1,128]{1,0:T(1,128)}, u32[]{:S(2)}) copy-start(s32[1,128]{1,0:T(1,128)} %param.21) | copy-start | bytes 1540
  13.6 92.6 %all-to-all-start = ((bf16[16,3,32,256]{3,2,1,0:T(8,128)(2,1)}), bf16[16,3,32,256]{3,2,1,0:T(8,128)(2,1)S(1)}, u32[]{:S(2)}, u32[]{:S(2)}) async-start(bf16[16,3,32,256]{3,2,1,0:T(8,128)(2,1)} %reshape.288), calls=%async_computation | async-start | bytes 1572864 | tf_op jit(solution)/shard_map/all_to_all | solution.py:113
  21.9 101.5 %all-gather.17.cloned.1.call-start = ((), (), s32[]{:S(2)}) async-start(), calls=%async_computation.11 | async-start | bytes 2359296 | tf_op jit(solution)/shard_map/all_gather | solution.py:114
  107.1 88.9 %all-gather.15.cloned.1.call-start = ((), (), s32[]{:S(2)}) async-start(), calls=%async_computation.10 | async-start | bytes 4456448 | tf_op jit(solution)/shard_map/all_gather | solution.py:42
  109.5 6.4 copy-start.26
  120.1 85.7 %all-gather.13.cloned.1.call-start = ((), (), s32[]{:S(2)}) async-start(), calls=%async_computation.6 | async-start | bytes 2359296 | tf_op jit(solution)/shard_map/all_gather | solution.py:117
  121.2 165.1 %all-gather.19.cloned.1.call-start = ((), (), s32[]{:S(2)}) async-start(), calls=%async_computation.12 | async-start | bytes 4456448 | tf_op jit(solution)/shard_map/all_gather | solution.py:42
  122.2 425.2 %reduce-scatter.15.cloned.1.call-start = ((), (), s32[]{:S(2)}) async-start(), calls=%async_computation.8 | async-start | bytes 4456448 | tf_op jit(solution)/shard_map/reduce_scatter | solution.py:46
  286.3 8.1 copy-start.4
  416.4 10.2 %copy-start.20 = (bf16[3,256,1024]{2,1,0:T(8,128)(2,1)S(1)}, bf16[3,256,1024]{2,1,0:T(8,128)(2,1)}, u32[]{:S(2)}) copy-start(bf16[3,256,1024]{2,1,0:T(8,128)(2,1)} %all-gather.13.cloned.1.call-done) | copy-start | bytes 4718596
  416.4 10.2 %copy-start.58 = (f32[1280,256]{1,0:T(8,128)S(1)}, f32[1280,256]{1,0:T(8,128)}, u32[]{:S(2)}) copy-start(f32[1280,256]{1,0:T(8,128)} %get-tuple-element.97) | copy-start | bytes 3932164
  445.1 6.2 slice-start.2
  445.1 6.2 slice-start.4
  445.1 6.2 slice-start.3
  454.3 94.8 %copy-start.14 = (bf16[128,1024]{1,0:T(8,128)(2,1)S(1)}, bf16[128,1024]{1,0:T(8,128)(2,1)}, u32[]{:S(2)}) copy-start(bf16[128,1024]{1,0:T(8,128)(2,1)} %convolution_convert_fusion.4) | copy-start | bytes 786436
  454.3 164.6 %all-reduce.14.cloned.1.call-start = ((), (), s32[]{:S(2)}) async-start(), calls=%async_computation.13 | async-start | bytes 16777216
  563.9 116.9 %reduce-scatter.17.cloned.1.call-start = ((), (), s32[]{:S(2)}) async-start(), calls=%async_computation.9 | async-start | bytes 4718592 | tf_op jit(solution)/shard_map/reduce_scatter | solution.py:214
  572.5 165.1 %reduce-scatter.13.cloned.1.call-start = ((), (), s32[]{:S(2)}) async-start(), calls=%async_computation.7 | async-start | bytes 4456448 | tf_op jit(solution)/shard_map/reduce_scatter | solution.py:46
  613.2 61.6 %all-to-all-start.1 = ((bf16[16,3,32,256]{3,2,1,0:T(8,128)(2,1)}), bf16[16,3,32,256]{3,2,1,0:T(8,128)(2,1)}, u32[]{:S(2)}, u32[]{:S(2)}) async-start(bf16[16,3,32,256]{3,2,1,0:T(8,128)(2,1)} %copy.104), calls=%async_computation.3 | async-start | bytes 1572864 | tf_op jit(solution)/shard_map/all_to_all | solution.py:217
  618.9 278.1 %all-reduce.16.cloned.1.call-start = ((), (), s32[]{:S(2)}) async-start(), calls=%async_computation.14 | async-start | bytes 8388608
  624.6 49.7 %copy-start.53 = (f32[2]{0:T(128)S(1)}, f32[2]{0:T(128)}, u32[]{:S(2)}) copy-start(f32[2]{0:T(128)} %param.39) | copy-start | bytes 28
  737.6 161.9 %copy-start.1 = (bf16[128,1024]{1,0:T(8,128)(2,1)S(1)}, bf16[128,1024]{1,0:T(8,128)(2,1)}, u32[]{:S(2)}) copy-start(bf16[128,1024]{1,0:T(8,128)(2,1)} %param.20) | copy-start | bytes 786436
  (45 other events, 132.0 us)
Sparse Core Ops, SparseCore 0:
  11.5 86.9 all-gather.10
  107.2 8.1 all-gather.16
  120.2 75.7 all-gather.14
  197.4 8.3 all-gather.12
  209.0 77.2 all-gather.18
  454.4 92.9 reduce-scatter.14
  564.0 38.4 all-reduce.13
  604.7 12.2 reduce-scatter.16
  619.4 101.9 reduce-scatter.12
  727.8 169.1 all-reduce.15
where the time goes:
time: 914 us; the launch traced here: 907 us
  waiting for transfers between devices  397 us (43%)
  blocking collectives  296 us (32%)
  matrix products  86.9 us (10%)
  local copies, waits for them, and re-layouts  55.6 us (6%)
  other arithmetic  40 us (4%)
  between operations  16.4 us (2%)
  starting transfers between devices  15.4 us (2%)
    unnamed x12, waiting for transfers between devices  157 us
    all_gather x2, waiting for transfers between devices, ag(): return lax.all_gather(block, 'shard', axis=0, tiled=False)  146 us
    reduce_scatter x2, waiting for transfers between devices, rs(): lax.psum_scatter(parts.astype(BF), 'shard', scatter_dimension=0, tiled=Fa...  92.5 us
    unnamed x2, blocking collectives  86.7 us
    all_gather x1, blocking collectives, body(): small = lax.all_gather(small, BOTH, axis=1, tiled=True)  81.6 us
    dot_general x35, matrix products, mm(): return lax.dot_general(a, b, (dims, ((), ())), preferred_element_type=F32)  80.9 us
    psum x1, blocking collectives, body(): counts = lax.psum(jnp.stack([n0, T - n0]), BOTH)  48.3 us
    psum x1, blocking collectives, body(): smalls = lax.psum(jnp.stack([gg1, gb1, gg2, gb2] + gw), BOTH)  43.1 us
  transfers between devices with their start and end apart: 12, of which 5 were waited for; matrix products, arithmetic and copies ran while one was open for 11% of the time, Pallas kernels for 0%

commit v1 on v0

--- a/solution.py
+++ b/solution.py
@@ -216,7 +216,7 @@
     gup = lax.psum_scatter(gup, "dp", scatter_dimension=0, tiled=False).astype(BF)
     gup = lax.all_to_all(gup, "shard", 0, 0).astype(F32)
     gup = gup.reshape(S, 3, WR, C, FR).transpose(1, 2, 3, 0, 4).reshape(3, WR, FF)
-    counts = lax.psum(jnp.stack([n0, T - n0]), BOTH)
+    counts = jnp.sum(lax.all_gather(jnp.stack([n0, T - n0]), BOTH), axis=0)
     load_new = 0.9 * load_avg + 0.1 * counts.astype(F32) * E / (T * C * S)
     return (
         layer_out,

time: 914 us -> 914 us (level)
    psum x1 -> x0, blocking collectives: 48.3 us -> none  [body(): counts = lax.psum(jnp.stack([n0, T - n0]), BOTH)]
    unnamed x2 -> x3, blocking collectives: 86.7 us -> 135 us
where the time goes in v1:
time: 914 us; the launch traced here: 907 us
  waiting for transfers between devices  397 us (43%)
  blocking collectives  296 us (32%)
  matrix products  86.9 us (10%)
  local copies, waits for them, and re-layouts  55.5 us (6%)
  other arithmetic  40.1 us (4%)
  between operations  16.5 us (2%)
  starting transfers between devices  15.5 us (2%)
    unnamed x12, waiting for transfers between devices  156 us
    all_gather x2, waiting for transfers between devices, ag(): return lax.all_gather(block, 'shard', axis=0, tiled=False)  146 us
    unnamed x3, blocking collectives  135 us
    reduce_scatter x2, waiting for transfers between devices, rs(): lax.psum_scatter(parts.astype(BF), 'shard', scatter_dimension=0, tiled=Fa...  92.5 us
    all_gather x1, blocking collectives, body(): small = lax.all_gather(small, BOTH, axis=1, tiled=True)  81.6 us
    dot_general x35, matrix products, mm(): return lax.dot_general(a, b, (dims, ((), ())), preferred_element_type=F32)  80.9 us
    psum x1, blocking collectives, body(): smalls = lax.psum(jnp.stack([gg1, gb1, gg2, gb2] + gw), BOTH)  43.5 us
    all_gather x1, blocking collectives, ag(): return lax.all_gather(block, 'shard', axis=0, tiled=False)  35.8 us
  transfers between devices with their start and end apart: 12, of which 5 were waited for; matrix products, arithmetic and copies ran while one was open for 11% of the time, Pallas kernels for 0%

profile of v1, /device:TPU:0, one launch (start us, length us, event | category | flops | bytes accessed | tf_op | source)
XLA Modules:
  0.0 906.8 jit_solution(3433247173874429231)
XLA Ops:
  13.6 8.3 all-to-all-start
  22.1 81.6 %all-gather.5 = f32[32,32,8]{1,2,0:T(8,128)S(1)} all-gather(f32[1,32,8]{1,2,0:T(8,128)S(1)} %convert_bitcast_fusion.4), channel_id=1, replica_groups=mesh['dp'=2,'shard'=16] {'dp','shard'}, dimensions={0}, use_global_device_ids=true | all-gather | bytes 33792 | tf_op jit(solution)/shard_map/all_gather | solution.py:105
  125.9 70.1 %all-gather.16.cloned.1.call-done = bf16[2048,1024]{1,0:T(8,128)(2,1)} async-done(((bf16[128,1024]{1,0:T(8,128)(2,1)}), bf16[2048,1024]{1,0:T(8,128)(2,1)}) %all-gather.16.cloned.1.call-update) | async-done | bytes 4194320 | tf_op jit(solution)/shard_map/all_gather | solution.py:42
  196.0 3.2 fusion.113
  199.2 2.8 multiply_convert_fusion.1
  205.8 4.4 fusion.52
  210.2 76.1 %all-gather.20.cloned.1.call-done = bf16[2048,1024]{1,0:T(8,128)(2,1)} async-done(((bf16[128,1024]{1,0:T(8,128)(2,1)}), bf16[2048,1024]{1,0:T(8,128)(2,1)}) %all-gather.20.cloned.1.call-update) | async-done | bytes 4194320 | tf_op jit(solution)/shard_map/all_gather | solution.py:42
  286.3 8.0 fusion.4
  294.4 2.9 multiply_convert_fusion
  297.4 6.0 fusion.2
  303.4 74.4 %all-reduce.7 = f32[16,3,128]{2,1,0:T(4,128)S(1)} all-reduce(f32[16,3,128]{2,1,0:T(4,128)S(1)} %pad_maximum_fusion.3), channel_id=9, replica_groups=mesh['dp'=2,'shard'=16] {'shard'}, use_global_device_ids=true, to_apply=%region_18.19.clone | all-reduce | flops 6144 | bytes 49152
  380.5 35.8 %all-gather.2 = f32[2048,3]{0,1:T(4,128)S(1)} all-gather(f32[128,3]{0,1:T(4,128)S(1)} %pad_maximum_fusion.4), channel_id=4, replica_groups=mesh['dp'=2,'shard'=16] {'shard'}, dimensions={0}, use_global_device_ids=true | all-gather | bytes 26112 | tf_op jit(solution)/shard_map/all_gather | solution.py:42
  416.4 10.2 %fusion.3 = (bf16[16,80,1024]{2,1,0:T(8,128)(2,1)S(1)}, bf16[16,80,1024]{2,1,0:T(8,128)(2,1)S(1)}, f32[16,80,1024]{2,1,0:T(8,128)}, f32[16,80,1024]{2,1,0:T(8,128)}) fusion(f32[16,80]{1,0:T(8,128)S(1)} %get-tuple-element.62, bf16[16,128,1024]{2,1,0:T(8,128)(2,1)} %bitcast.390, f32[16,80]{1,0:T(8,128)S(1)} %get-tuple-element.63, f32[16,80,1024]{2,1,0:T(8,128)} %fusion.52, ...), kind=kLoop, calls=%fused_computation.12 | loop fusion | flops 10485760 | bytes 31467520 | tf_op jit(solution)/shard_map/convert_element_type | solution.py:163
  428.1 3.2 fusion.119
  432.7 3.5 fusion.120
  438.2 7.0 fusion.1
  445.2 5.2 fusion.7
  451.4 2.9 add_convert_fusion
  455.0 92.5 %reduce-scatter.15.cloned.1.call-done = bf16[1,128,1024]{2,1,0:T(8,128)(2,1)} async-done(((bf16[16,128,1024]{2,1,0:T(8,128)(2,1)}), bf16[1,128,1024]{2,1,0:T(8,128)(2,1)}) %reduce-scatter.15.cloned.1.call-update) | async-done | bytes 262160 | tf_op jit(solution)/shard_map/reduce_scatter | solution.py:46
  560.1 3.8 maximum_bitcast_fusion
  564.0 3.0 convolution_bitcast_fusion
  574.1 4.6 copy.102
  578.7 4.4 copy.103
  583.1 6.5 copy.101
  589.7 3.3 convolution_bitcast_fusion.4
  599.2 12.2 %all-reduce.18 = bf16[2,16,3,32,256]{4,3,1,0,2:T(8,128)(2,1)S(1)} all-reduce(f32[2,16,3,32,256]{4,3,1,0,2:T(8,128)} %maximum_bitcast_fusion.1), channel_id=12, replica_groups=mesh['dp'=2,'shard'=16] {'dp'}, use_global_device_ids=true, to_apply=%region_35.36.clone | all-reduce | flops 786432 | bytes 4718592
  613.1 5.8 all-to-all-start.1
  619.0 5.6 dynamic-slice_bitcast_fusion
  626.1 48.2 %all-reduce.6 = s32[64]{0:T(128)S(1)} all-reduce(s32[64]{0:T(128)S(1)} %add_dynamic-update-slice_fusion), channel_id=6, replica_groups=mesh['dp'=2,'shard'=16] {'dp','shard'}, use_global_device_ids=true, to_apply=%add.6 | all-reduce | flops 64 | bytes 512
  690.2 2.6 multiply_reduce_fusion.6
  692.8 43.5 %psum.7 = f32[8,1024]{1,0:T(8,128)S(1)} all-reduce(f32[8,1024]{1,0:T(8,128)S(1)} %stack.176), channel_id=1, replica_groups=mesh['dp'=2,'shard'=16] {'dp','shard'}, use_global_device_ids=true, to_apply=%region_32.33 | all-reduce | flops 8192 | bytes 65536 | tf_op jit(solution)/shard_map/psum | solution.py:209
  741.2 155.9 %all-reduce.17.cloned.1.call-done = bf16[16,4,32,1024]{3,2,0,1:T(8,128)(2,1)} async-done(((bf16[16,4,32,1024]{3,2,0,1:T(8,128)(2,1)}), bf16[16,4,32,1024]{3,2,0,1:T(8,128)(2,1)}) %all-reduce.17.cloned.1.call-update) | async-done | bytes 4194320
  (274 shorter events, 92.7 us)
Async XLA Ops:
  7.2 98.4 %copy-start = (bf16[128,1024]{1,0:T(8,128)(2,1)S(1)}, bf16[128,1024]{1,0:T(8,128)(2,1)}, u32[]{:S(2)}) copy-start(bf16[128,1024]{1,0:T(8,128)(2,1)} %param.20) | copy-start | bytes 786436
  7.2 100.0 %all-gather.12.cloned.1.call-start = ((), (), s32[]{:S(2)}) async-start(), calls=%async_computation.5 | async-start | bytes 8650752 | tf_op jit(solution)/shard_map/all_gather | solution.py:109
  11.0 10.9 %copy-start.44 = (bf16[32,2]{0,1:T(2,128)(2,1)S(1)}, bf16[32,2]{0,1:T(2,128)(2,1)}, u32[]{:S(2)}) copy-start(bf16[32,2]{0,1:T(2,128)(2,1)} %param.36) | copy-start | bytes 388
  11.1 10.9 %copy-start.45 = (bf16[32,2]{0,1:T(2,128)(2,1)S(1)}, bf16[32,2]{0,1:T(2,128)(2,1)}, u32[]{:S(2)}) copy-start(bf16[32,2]{0,1:T(2,128)(2,1)} %param.35) | copy-start | bytes 388
  11.1 10.9 %copy-start.46 = (bf16[32]{0:T(256)(128)(2,1)S(1)}, bf16[32]{0:T(256)(128)(2,1)}, u32[]{:S(2)}) copy-start(bf16[32]{0:T(256)(128)(2,1)} %param.25) | copy-start | bytes 196
  11.1 10.9 %copy-start.47 = (bf16[32]{0:T(256)(128)(2,1)S(1)}, bf16[32]{0:T(256)(128)(2,1)}, u32[]{:S(2)}) copy-start(bf16[32]{0:T(256)(128)(2,1)} %param.26) | copy-start | bytes 196
  11.1 10.9 %copy-start.48 = (bf16[32]{0:T(256)(128)(2,1)S(1)}, bf16[32]{0:T(256)(128)(2,1)}, u32[]{:S(2)}) copy-start(bf16[32]{0:T(256)(128)(2,1)} %param.31) | copy-start | bytes 196
  11.1 10.9 %copy-start.49 = (bf16[32]{0:T(256)(128)(2,1)S(1)}, bf16[32]{0:T(256)(128)(2,1)}, u32[]{:S(2)}) copy-start(bf16[32]{0:T(256)(128)(2,1)} %param.32) | copy-start | bytes 196
  12.1 91.7 %copy-start.52 = (s32[128]{0:T(128)S(1)}, s32[128]{0:T(128)}, u32[]{:S(2)}) copy-start(s32[128]{0:T(128)} %param.22) | copy-start | bytes 1540
  12.2 92.3 %copy-start.51 = (s32[128]{0:T(128)S(1)}, s32[128]{0:T(128)}, u32[]{:S(2)}) copy-start(s32[128]{0:T(128)} %param.23) | copy-start | bytes 1540
  12.2 93.0 %copy-start.53 = (s32[1,128]{1,0:T(1,128)S(1)}, s32[1,128]{1,0:T(1,128)}, u32[]{:S(2)}) copy-start(s32[1,128]{1,0:T(1,128)} %param.21) | copy-start | bytes 1540
  13.6 92.6 %all-to-all-start = ((bf16[16,3,32,256]{3,2,1,0:T(8,128)(2,1)}), bf16[16,3,32,256]{3,2,1,0:T(8,128)(2,1)S(1)}, u32[]{:S(2)}, u32[]{:S(2)}) async-start(bf16[16,3,32,256]{3,2,1,0:T(8,128)(2,1)} %reshape.288), calls=%async_computation | async-start | bytes 1572864 | tf_op jit(solution)/shard_map/all_to_all | solution.py:113
  21.9 101.5 %all-gather.18.cloned.1.call-start = ((), (), s32[]{:S(2)}) async-start(), calls=%async_computation.11 | async-start | bytes 2359296 | tf_op jit(solution)/shard_map/all_gather | solution.py:114
  107.1 88.9 %all-gather.16.cloned.1.call-start = ((), (), s32[]{:S(2)}) async-start(), calls=%async_computation.10 | async-start | bytes 4456448 | tf_op jit(solution)/shard_map/all_gather | solution.py:42
  109.5 6.4 copy-start.26
  120.1 85.7 %all-gather.14.cloned.1.call-start = ((), (), s32[]{:S(2)}) async-start(), calls=%async_computation.6 | async-start | bytes 2359296 | tf_op jit(solution)/shard_map/all_gather | solution.py:117
  121.2 165.1 %all-gather.20.cloned.1.call-start = ((), (), s32[]{:S(2)}) async-start(), calls=%async_computation.12 | async-start | bytes 4456448 | tf_op jit(solution)/shard_map/all_gather | solution.py:42
  122.2 425.2 %reduce-scatter.15.cloned.1.call-start = ((), (), s32[]{:S(2)}) async-start(), calls=%async_computation.8 | async-start | bytes 4456448 | tf_op jit(solution)/shard_map/reduce_scatter | solution.py:46
  286.3 8.1 copy-start.4
  416.4 10.2 %copy-start.20 = (bf16[3,256,1024]{2,1,0:T(8,128)(2,1)S(1)}, bf16[3,256,1024]{2,1,0:T(8,128)(2,1)}, u32[]{:S(2)}) copy-start(bf16[3,256,1024]{2,1,0:T(8,128)(2,1)} %all-gather.14.cloned.1.call-done) | copy-start | bytes 4718596
  416.4 10.2 %copy-start.58 = (f32[1280,256]{1,0:T(8,128)S(1)}, f32[1280,256]{1,0:T(8,128)}, u32[]{:S(2)}) copy-start(f32[1280,256]{1,0:T(8,128)} %get-tuple-element.97) | copy-start | bytes 3932164
  445.2 6.2 slice-start.2
  445.2 6.2 slice-start.4
  445.2 6.2 slice-start.3
  454.4 94.8 %copy-start.14 = (bf16[128,1024]{1,0:T(8,128)(2,1)S(1)}, bf16[128,1024]{1,0:T(8,128)(2,1)}, u32[]{:S(2)}) copy-start(bf16[128,1024]{1,0:T(8,128)(2,1)} %convolution_convert_fusion.4) | copy-start | bytes 786436
  454.4 164.6 %all-reduce.15.cloned.1.call-start = ((), (), s32[]{:S(2)}) async-start(), calls=%async_computation.13 | async-start | bytes 16777216
  563.9 117.1 %reduce-scatter.17.cloned.1.call-start = ((), (), s32[]{:S(2)}) async-start(), calls=%async_computation.9 | async-start | bytes 4718592 | tf_op jit(solution)/shard_map/reduce_scatter | solution.py:214
  572.6 165.5 %reduce-scatter.13.cloned.1.call-start = ((), (), s32[]{:S(2)}) async-start(), calls=%async_computation.7 | async-start | bytes 4456448 | tf_op jit(solution)/shard_map/reduce_scatter | solution.py:46
  613.1 61.9 %all-to-all-start.1 = ((bf16[16,3,32,256]{3,2,1,0:T(8,128)(2,1)}), bf16[16,3,32,256]{3,2,1,0:T(8,128)(2,1)}, u32[]{:S(2)}, u32[]{:S(2)}) async-start(bf16[16,3,32,256]{3,2,1,0:T(8,128)(2,1)} %copy.104), calls=%async_computation.3 | async-start | bytes 1572864 | tf_op jit(solution)/shard_map/all_to_all | solution.py:217
  618.9 278.1 %all-reduce.17.cloned.1.call-start = ((), (), s32[]{:S(2)}) async-start(), calls=%async_computation.14 | async-start | bytes 8388608
  624.6 49.9 %copy-start.54 = (f32[2]{0:T(128)S(1)}, f32[2]{0:T(128)}, u32[]{:S(2)}) copy-start(f32[2]{0:T(128)} %param.39) | copy-start | bytes 28
  738.1 161.4 %copy-start.1 = (bf16[128,1024]{1,0:T(8,128)(2,1)S(1)}, bf16[128,1024]{1,0:T(8,128)(2,1)}, u32[]{:S(2)}) copy-start(bf16[128,1024]{1,0:T(8,128)(2,1)} %param.20) | copy-start | bytes 786436
  (45 other events, 131.9 us)
Sparse Core Ops, SparseCore 0:
  11.5 86.9 all-gather.11
  107.2 8.1 all-gather.17
  120.2 75.7 all-gather.15
  197.4 8.3 all-gather.13
  209.0 77.2 all-gather.19
  454.5 92.9 reduce-scatter.14
  564.0 38.4 all-reduce.14
  604.7 12.2 reduce-scatter.16
  619.5 101.9 reduce-scatter.12
  727.9 169.1 all-reduce.16
